TPU v7x, 512 devices: a whole 4x4x16 slice. The times are simulated.
512 devices in a mesh: frame: 16 (over z), dom: 8 (over x, core), coef: 4 (over y).
Axes of the slice: x: 4, y: 4, z: 16, core: 2. Of those that a mesh axis runs over, the one named last changes fastest.
Arguments:
- geometry: float32 [32, 524288], P('coef', ('frame', 'dom')), may hold values from -1 to 1
- fraction: float32 [32, 524288], P('coef', ('frame', 'dom')), may hold values from 0 to 1
- interval: int32 [32, 524288], P('coef', ('frame', 'dom')), may hold values from 0 to 156
- pattern: int32 [32, 4096], P('coef', ('frame', 'dom')), may hold values from 0 to 95
- target: float32 [524288], P(('frame', 'dom')), may hold values from -8 to 8
Outputs:
- solution: float32 [384, 160], P('coef')
- residual: float32 [524288], P(('frame', 'dom'))
Inputs may be any that keep to these rules, and one draw needn't show every extreme that they name: The spline of a slot reads coefficients interval to interval + 3 of its type. Slot s refers to pair type (s // 8) * 96 + pattern.
All inputs are finite; a program needn't handle non-finite values.
Results may differ from a plain program's by a relative error of at most 0.0003.
Values sent between devices are 32-bit elements; how exact they have to be, the bound alone decides.
No kernel may reach another device: no remote copies, remote signals or barrier semaphores. Data moves between devices by JAX's collectives and lax.ppermute only.
A program may use at most 64 MiB of HBM per device.

v0:
```python
import math
import jax
import jax.numpy as jnp
from jax import lax
from jax.sharding import PartitionSpec as P

NK = 160
TYPES = 384
ITERS = 2


def spline_weights(fraction):
    square = fraction * fraction
    cube = square * fraction
    return (
        (1.0 - fraction) ** 3 / 6.0,
        (3.0 * cube - 6.0 * square + 4.0) / 6.0,
        (-3.0 * cube + 3.0 * square + 3.0 * fraction + 1.0) / 6.0,
        cube / 6.0,
    )


def dense_tiles(geom, fraction, interval):
    knots = lax.broadcasted_iota(jnp.int32, (1, NK, 1), 1)
    tiles = jnp.zeros((geom.shape[0], NK, geom.shape[1]), jnp.float32)
    for offset, weight in enumerate(spline_weights(fraction)):
        hit = knots == (interval + offset)[:, None, :]
        tiles = tiles + jnp.where(hit, (geom * weight)[:, None, :], 0.0)
    return tiles


def block_layout(geom):
    tiles_all = geom.shape[1] // 128
    block = math.gcd(8, tiles_all)
    return (block, block * 128, tiles_all // block)


def block_tiles(geometry, fraction, interval, pattern, index, block, width):
    start = index * width
    geom = lax.dynamic_slice_in_dim(geometry, start, width, 1)
    frac = lax.dynamic_slice_in_dim(fraction, start, width, 1)
    knot = lax.dynamic_slice_in_dim(interval, start, width, 1)
    kinds = lax.dynamic_slice_in_dim(pattern, index * block, block, 1)
    tiles = dense_tiles(geom, frac, knot).reshape(geom.shape[0], NK, block, 128)
    return (tiles, kinds, start)


def forward(coeffs, geometry, fraction, interval, pattern):
    block, width, count = block_layout(geometry)

    def forward_step(index, image):
        tiles, kinds, start = block_tiles(
            geometry, fraction, interval, pattern, index, block, width
        )
        chosen = jnp.take(coeffs, kinds, axis=0)
        part = jnp.einsum("sktr,stk->tr", tiles, chosen, precision=lax.Precision.HIGHEST)
        return lax.dynamic_update_slice_in_dim(image, part.reshape(width), start, 0)

    return lax.fori_loop(0, count, forward_step, jnp.zeros((geometry.shape[1],), jnp.float32))


def backward(resid, per_coef, geometry, fraction, interval, pattern):
    block, width, count = block_layout(geometry)
    owners = lax.broadcasted_iota(jnp.int32, (1, 1, per_coef), 2)

    def backward_step(index, total):
        tiles, kinds, start = block_tiles(
            geometry, fraction, interval, pattern, index, block, width
        )
        piece = lax.dynamic_slice_in_dim(resid, start, width, 0).reshape(block, 128)
        contrib = jnp.einsum("sktr,tr->stk", tiles, piece, precision=lax.Precision.HIGHEST)
        picks = (kinds[:, :, None] == owners).astype(jnp.float32)
        return total + jnp.einsum("stc,stk->ck", picks, contrib, precision=lax.Precision.HIGHEST)

    return lax.fori_loop(0, count, backward_step, jnp.zeros((per_coef, NK), jnp.float32))


def on_device(geometry, fraction, interval, pattern, target):
    per_coef = TYPES // lax.axis_size("coef")

    def transpose_sum(resid):
        local = backward(resid, per_coef, geometry, fraction, interval, pattern).reshape(
            per_coef * NK
        )
        share = lax.psum(local, ("frame", "dom"))
        total = lax.psum(jnp.sum(share * share), "coef")
        return (share, total)

    def expand(share):
        return share.reshape(per_coef, NK)

    residual = target
    gradient, gamma = transpose_sum(residual)
    direction = gradient
    solution = jnp.zeros_like(gradient)
    for step_index in range(ITERS):
        partial_image = forward(expand(direction), geometry, fraction, interval, pattern)
        image = lax.psum(partial_image, "coef")
        image_total = lax.psum(jnp.sum(image * image), ("frame", "dom"))
        alpha = gamma / image_total
        solution = solution + alpha * direction
        residual = residual - alpha * image
        if step_index + 1 < ITERS:
            gradient, gamma_next = transpose_sum(residual)
            direction = gradient + gamma_next / gamma * direction
            gamma = gamma_next
    return (expand(solution), residual)


def solution(mesh):
    in_specs = (
        P("coef", ("frame", "dom")),
        P("coef", ("frame", "dom")),
        P("coef", ("frame", "dom")),
        P("coef", ("frame", "dom")),
        P(("frame", "dom")),
    )
    out_specs = (P("coef", None), P(("frame", "dom")))
    return jax.shard_map(
        on_device, mesh=mesh, in_specs=in_specs, out_specs=out_specs, check_vma=False
    )
```

profile of v0, /device:TPU:1, one launch (start us, length us, event | category | flops | bytes accessed | tf_op | source)
XLA Modules:
  0.0 1750.1 jit_solution(9884929640221820795)
XLA Ops:
  0.6 52.4 %while.56 = (s32[]{:T(128)}, f32[96,160]{0,1:T(8,128)S(1)}, s32[8,32]{1,0:T(8,128)}, f32[4096]{0:T(1024)}, s32[8,4096]{1,0:T(8,128)}, /*index=5*/f32[8,4096]{1,0...) while((s32[]{:T(128)}, f32[96,160]{0,1:T(8,128)S(1)}, ...), condition=%wide.region_1.2_spmd.clone, body=%wide.region_0.1_spmd.clone.sunk | while | flops 42192900 | bytes 11854863 | solution.py:75
  5.0 8.4 fusion.118
  18.1 8.4 fusion.118
  31.2 8.4 fusion.118
  44.3 8.4 fusion.118
  53.3 498.0 %psum.56 = f32[15360]{0:T(1024)S(1)} all-reduce(f32[15360]{0:T(1024)S(1)} %reshape.226), channel_id=1, replica_groups=mesh['frame'=16,'dom'=8,'coef'=4] {'frame','dom'}, use_global_device_ids=true, to_apply=%region_2.3 | all-reduce | flops 15360 | bytes 122880 | tf_op jit(solution)/shard_map/psum | solution.py:85
  551.4 53.3 %while.54 = (s32[]{:T(128)}, f32[4096]{0:T(1024)S(1)}, s32[8,4096]{1,0:T(8,128)}, f32[8,4096]{1,0:T(8,128)}, f32[8,4096]{1,0:T(8,128)}, /*index=5*/s32[8,32]{1,0...) while((s32[]{:T(128)}, f32[4096]{0:T(1024)S(1)}, ...), condition=%wide.region_6.0_spmd, body=%wide.region_5.7_spmd.sunk | while | flops 30371208 | bytes 11859845 | solution.py:59
  558.3 6.1 fusion.108
  571.6 6.1 fusion.108
  598.3 6.1 fusion.108
  605.3 14.6 all-reduce
  620.5 256.4 %psum.59 = f32[]{:T(128)} all-reduce(f32[]{:T(128)} %multiply_reduce_fusion.3), channel_id=1, replica_groups=mesh['frame'=16,'dom'=8,'coef'=4] {'frame','dom'}, use_global_device_ids=true, to_apply=%region_9.11 | all-reduce | flops 1 | bytes 8 | tf_op jit(solution)/shard_map/psum | solution.py:99
  878.3 49.7 %while.57 = (s32[]{:T(128)}, f32[96,160]{0,1:T(8,128)S(1)}, s32[8,32]{1,0:T(8,128)}, f32[4096]{0:T(1024)S(1)}, s32[8,4096]{1,0:T(8,128)}, /*index=5*/f32[8,4096]...) while((s32[]{:T(128)}, f32[96,160]{0,1:T(8,128)S(1)}, ...), condition=%wide.region_11.13_spmd.clone, body=%wide.region_10.12_spmd.clone.sunk | while | flops 42192900 | bytes 11854863 | solution.py:75
  882.0 8.4 fusion.124
  894.4 8.4 fusion.124
  906.9 8.4 fusion.124
  919.3 8.4 fusion.124
  928.3 485.9 %psum.60 = f32[15360]{0:T(1024)S(1)} all-reduce(f32[15360]{0:T(1024)S(1)} %reshape.228), channel_id=1, replica_groups=mesh['frame'=16,'dom'=8,'coef'=4] {'frame','dom'}, use_global_device_ids=true, to_apply=%region_12.14 | all-reduce | flops 15360 | bytes 122880 | tf_op jit(solution)/shard_map/psum | solution.py:85
  1414.8 6.9 psum.61
  1423.1 53.3 %while.55 = (s32[]{:T(128)}, f32[4096]{0:T(1024)S(1)}, s32[8,4096]{1,0:T(8,128)}, f32[8,4096]{1,0:T(8,128)}, f32[8,4096]{1,0:T(8,128)}, /*index=5*/s32[8,32]{1,0...) while((s32[]{:T(128)}, f32[4096]{0:T(1024)S(1)}, ...), condition=%wide.region_16.18_spmd, body=%wide.region_15.17_spmd.sunk | while | flops 30371208 | bytes 11859845 | solution.py:59
  1430.0 6.1 fusion.113
  1456.6 6.1 fusion.113
  1476.4 12.1 psum.62
  1489.1 258.2 %psum.63 = f32[]{:T(128)} all-reduce(f32[]{:T(128)} %multiply_reduce_fusion.2), channel_id=1, replica_groups=mesh['frame'=16,'dom'=8,'coef'=4] {'frame','dom'}, use_global_device_ids=true, to_apply=%region_19.21 | all-reduce | flops 1 | bytes 8 | tf_op jit(solution)/shard_map/psum | solution.py:99
  (305 shorter events, 114.0 us)
Async XLA Ops:
  4.3 9.1 copy-start
  17.4 9.1 copy-start
  30.5 9.1 copy-start
  43.6 9.1 copy-start
  551.4 326.9 %copy-start.4 = (f32[4096]{0:T(1024)S(1)}, f32[4096]{0:T(1024)}, u32[]{:S(2)}) copy-start(f32[4096]{0:T(1024)} %get-tuple-element.1094) | copy-start | bytes 49156
  551.4 6.0 copy-start.1
  564.8 6.0 copy-start.1
  578.1 6.0 copy-start.1
  591.4 6.0 copy-start.1
  882.0 8.4 copy-start.2
  894.4 8.4 copy-start.2
  906.8 8.4 copy-start.2
  919.3 8.4 copy-start.2
  1423.1 6.0 copy-start.3
  1436.4 6.0 copy-start.3
  1449.8 6.0 copy-start.3
  1463.1 6.0 copy-start.3
where the time goes:
time: 1750 us
  blocking collectives  1530 us (87%)
  matrix products  118 us (7%)
  other arithmetic  78.9 us (5%)
    psum x2, blocking collectives, transpose_sum(): share = lax.psum(local, ('frame', 'dom'))  984 us
    psum x2, blocking collectives, on_device(): image_total = lax.psum(jnp.sum(image * image), ('frame', 'dom'))  515 us
    dot_general x8, matrix products, backward_step(): jnp.einsum('sktr,tr->stk', tiles, piece, precision=lax.Precision.HIGHEST)  66.9 us
    add x16, other arithmetic, dense_tiles(): tiles = tiles + jnp.where(hit, (geom * weight)[:, None, :], 0.0)  49.2 us
    dot_general x8, matrix products, forward_step(): jnp.einsum('sktr,stk->tr', tiles, chosen, precision=lax.Precision.HIGHEST)  49 us

commit v1 on v0

--- a/solution.py
+++ b/solution.py
@@ -82,7 +82,7 @@
         local = backward(resid, per_coef, geometry, fraction, interval, pattern).reshape(
             per_coef * NK
         )
-        share = lax.psum(local, ("frame", "dom"))
+        share = lax.psum(lax.psum(local, "frame"), "dom")
         total = lax.psum(jnp.sum(share * share), "coef")
         return (share, total)
 

time: 1750 us -> 923 us (0.53)
  blocking collectives: 1530 us -> 702 us
    psum x2 -> x4, blocking collectives: 984 us -> 159 us  [transpose_sum(): share = lax.psum(lax.psum(local, 'frame'), 'dom')]
where the time goes in v1:
time: 923 us; the launch traced here: 920 us
  blocking collectives  702 us (76%)
  matrix products  118 us (13%)
  other arithmetic  78.9 us (9%)
  local copies, waits for them, and re-layouts  14.3 us (2%)
    psum x2, blocking collectives, on_device(): image_total = lax.psum(jnp.sum(image * image), ('frame', 'dom'))  510 us
    psum x4, blocking collectives, transpose_sum(): share = lax.psum(lax.psum(local, 'frame'), 'dom')  159 us
    dot_general x8, matrix products, backward_step(): jnp.einsum('sktr,tr->stk', tiles, piece, precision=lax.Precision.HIGHEST)  66.9 us
    add x16, other arithmetic, dense_tiles(): tiles = tiles + jnp.where(hit, (geom * weight)[:, None, :], 0.0)  49.2 us
    dot_general x8, matrix products, forward_step(): jnp.einsum('sktr,stk->tr', tiles, chosen, precision=lax.Precision.HIGHEST)  49 us
    psum x2, blocking collectives, on_device(): image = lax.psum(partial_image, 'coef')  27.1 us

profile of v1, /device:TPU:1, one launch (start us, length us, event | category | flops | bytes accessed | tf_op | source)
XLA Modules:
  0.0 920.1 jit_solution(1691553866125200107)
XLA Ops:
  0.6 52.4 %while.56 = (s32[]{:T(128)}, f32[96,160]{0,1:T(8,128)S(1)}, s32[8,32]{1,0:T(8,128)}, f32[4096]{0:T(1024)}, s32[8,4096]{1,0:T(8,128)}, /*index=5*/f32[8,4096]{1,0...) while((s32[]{:T(128)}, f32[96,160]{0,1:T(8,128)S(1)}, ...), condition=%wide.region_1.2_spmd.clone, body=%wide.region_0.1_spmd.clone.sunk | while | flops 42192900 | bytes 11854863 | solution.py:75
  5.0 8.4 fusion.118
  18.1 8.4 fusion.118
  31.2 8.4 fusion.118
  44.3 8.4 fusion.118
  53.3 49.2 %psum.70 = f32[15360]{0:T(1024)S(1)} all-reduce(f32[15360]{0:T(1024)S(1)} %reshape.226), channel_id=1, replica_groups=mesh['frame'=16,'dom'=8,'coef'=4] {'frame'}, use_global_device_ids=true, to_apply=%region_2.3 | all-reduce | flops 15360 | bytes 122880 | tf_op jit(solution)/shard_map/psum | solution.py:85
  102.5 35.2 %psum.71 = f32[15360]{0:T(1024)S(1)} all-reduce(f32[15360]{0:T(1024)S(1)} %psum.70), channel_id=1, replica_groups=mesh['frame'=16,'dom'=8,'coef'=4] {'dom'}, use_global_device_ids=true, to_apply=%region_3.4 | all-reduce | flops 15360 | bytes 122880 | tf_op jit(solution)/shard_map/psum | solution.py:85
  137.8 53.3 %while.54 = (s32[]{:T(128)}, f32[4096]{0:T(1024)S(1)}, s32[8,4096]{1,0:T(8,128)}, f32[8,4096]{1,0:T(8,128)}, f32[8,4096]{1,0:T(8,128)}, /*index=5*/s32[8,32]{1,0...) while((s32[]{:T(128)}, f32[4096]{0:T(1024)S(1)}, ...), condition=%wide.region_7.0_spmd, body=%wide.region_6.8_spmd.sunk | while | flops 30371208 | bytes 11859845 | solution.py:59
  144.7 6.1 fusion.108
  171.4 6.1 fusion.108
  184.7 6.1 fusion.108
  191.7 15.0 %all-reduce = (f32[4096]{0:T(1024)S(1)}, f32[]{:T(128)}) all-reduce(f32[4096]{0:T(1024)S(1)} %get-tuple-element.530, f32[]{:T(128)} %multiply_reduce_fusion.1), channel_id=1, replica_groups=mesh['frame'=16,'dom'=8,'coef'=4] {'coef'}, use_global_device_ids=true, to_apply=%region_8.10 | all-reduce | flops 4097 | bytes 32776 | tf_op jit(solution)/shard_map/psum | solution.py:98
  207.3 253.8 %psum.74 = f32[]{:T(128)} all-reduce(f32[]{:T(128)} %multiply_reduce_fusion.3), channel_id=1, replica_groups=mesh['frame'=16,'dom'=8,'coef'=4] {'frame','dom'}, use_global_device_ids=true, to_apply=%region_10.12 | all-reduce | flops 1 | bytes 8 | tf_op jit(solution)/shard_map/psum | solution.py:99
  462.5 49.7 %while.57 = (s32[]{:T(128)}, f32[96,160]{0,1:T(8,128)S(1)}, s32[8,32]{1,0:T(8,128)}, f32[4096]{0:T(1024)S(1)}, s32[8,4096]{1,0:T(8,128)}, /*index=5*/f32[8,4096]...) while((s32[]{:T(128)}, f32[96,160]{0,1:T(8,128)S(1)}, ...), condition=%wide.region_12.14_spmd.clone, body=%wide.region_11.13_spmd.clone.sunk | while | flops 42192900 | bytes 11854863 | solution.py:75
  466.2 8.4 fusion.124
  478.6 8.4 fusion.124
  491.0 8.4 fusion.124
  503.5 8.4 fusion.124
  512.4 39.3 %psum.75 = f32[15360]{0:T(1024)S(1)} all-reduce(f32[15360]{0:T(1024)S(1)} %reshape.228), channel_id=1, replica_groups=mesh['frame'=16,'dom'=8,'coef'=4] {'frame'}, use_global_device_ids=true, to_apply=%region_13.15 | all-reduce | flops 15360 | bytes 122880 | tf_op jit(solution)/shard_map/psum | solution.py:85
  551.8 34.9 %psum.76 = f32[15360]{0:T(1024)S(1)} all-reduce(f32[15360]{0:T(1024)S(1)} %psum.75), channel_id=1, replica_groups=mesh['frame'=16,'dom'=8,'coef'=4] {'dom'}, use_global_device_ids=true, to_apply=%region_14.16 | all-reduce | flops 15360 | bytes 122880 | tf_op jit(solution)/shard_map/psum | solution.py:85
  587.3 6.9 psum.77
  595.6 53.3 %while.55 = (s32[]{:T(128)}, f32[4096]{0:T(1024)S(1)}, s32[8,4096]{1,0:T(8,128)}, f32[8,4096]{1,0:T(8,128)}, f32[8,4096]{1,0:T(8,128)}, /*index=5*/s32[8,32]{1,0...) while((s32[]{:T(128)}, f32[4096]{0:T(1024)S(1)}, ...), condition=%wide.region_18.20_spmd, body=%wide.region_17.19_spmd.sunk | while | flops 30371208 | bytes 11859845 | solution.py:59
  648.9 12.1 %psum.78 = f32[4096]{0:T(1024)S(1)} all-reduce(f32[4096]{0:T(1024)S(1)} %get-tuple-element.532), channel_id=1, replica_groups=mesh['frame'=16,'dom'=8,'coef'=4] {'coef'}, use_global_device_ids=true, to_apply=%region_19.21 | all-reduce | flops 4096 | bytes 32768 | tf_op jit(solution)/shard_map/psum | solution.py:98
  661.6 255.7 %psum.79 = f32[]{:T(128)} all-reduce(f32[]{:T(128)} %multiply_reduce_fusion.2), channel_id=1, replica_groups=mesh['frame'=16,'dom'=8,'coef'=4] {'frame','dom'}, use_global_device_ids=true, to_apply=%region_21.23 | all-reduce | flops 1 | bytes 8 | tf_op jit(solution)/shard_map/psum | solution.py:99
  (307 shorter events, 126.2 us)
Async XLA Ops:
  4.3 9.1 copy-start
  17.4 9.1 copy-start
  30.5 9.1 copy-start
  43.6 9.1 copy-start
  137.8 324.6 %copy-start.4 = (f32[4096]{0:T(1024)S(1)}, f32[4096]{0:T(1024)}, u32[]{:S(2)}) copy-start(f32[4096]{0:T(1024)} %get-tuple-element.1094) | copy-start | bytes 49156
  137.9 6.0 copy-start.1
  151.2 6.0 copy-start.1
  164.5 6.0 copy-start.1
  177.8 6.0 copy-start.1
  466.1 8.4 copy-start.2
  478.6 8.4 copy-start.2
  491.0 8.4 copy-start.2
  503.4 8.4 copy-start.2
  595.6 6.0 copy-start.3
  608.9 6.0 copy-start.3
  622.3 6.0 copy-start.3
  635.6 6.0 copy-start.3
